TPU v7x, 32 devices: a whole 2x2x4 slice. The times are simulated.
32 devices in a mesh: grp: 2 (over y), freq: 4 (over z), ell: 2 (over x), pol: 2 (over core).
Axes of the slice: x: 2, y: 2, z: 4, core: 2. Of those that a mesh axis runs over, the one named last changes fastest.
Arguments:
- beam_matrix: bfloat16 [8, 2, 512, 8192], P(('grp', 'freq'), None, None, ('ell', 'pol')), parts along dimension 0, may hold values from -0.375 to 0.375
- sky_spectrum: float32 [8, 3, 8192], P(('grp', 'freq'), None, ('ell', 'pol')), parts along dimension 0, may hold values from 0.1 to 10
- taper_tiles: bfloat16 [3, 512, 512], P(None, ('ell', 'pol')), may hold values from 0.5 to 1.5
- noise_tiles: bfloat16 [8, 3, 512, 2, 512], P(('grp', 'freq'), None, ('ell', 'pol')), parts along dimension 0, may hold values from -4 to 4
Outputs:
- covariance: float32 [8, 3, 512, 2, 512], P(('grp', 'freq'), None, ('ell', 'pol')), parts along dimension 0
There are 2 independent parts, one for each index of `grp`. A program takes and returns all parts, laid end to end along the dimension named above; an argument that names none is the same for every part. Nothing has to cross between parts.
All inputs are finite; a program needn't handle non-finite values.
Results may differ from a plain program's by a relative error of at most 0.012.
Values may be sent and summed in bfloat16 or wider, within the bound.
A program may use at most 64 MiB of HBM per device.

v0:
```python
import functools

import jax
import jax.numpy as jnp
from jax import lax
from jax.experimental import pallas as pl
from jax.experimental.pallas import tpu as pltpu
from jax.sharding import PartitionSpec as P

CHUNKS = 4
LANES = 128


def passed_along(block, axis, distance):
    devices = range(lax.axis_size(axis))
    route = [(i - distance, i) for i in devices if i - distance in devices]
    return lax.ppermute(block, axis, route)


def general_sums(beam_matrix, sky_spectrum, local_rows):
    per_device = beam_matrix.shape[0]
    mode_count = beam_matrix.shape[2]
    separations = sky_spectrum.shape[1]
    needed = (per_device - 1 + separations) // per_device
    blocks = [beam_matrix]
    for offset in range(needed):
        blocks.append(passed_along(beam_matrix, "freq", -(offset + 1)))
    term_list = []
    for sep_index in range(separations):
        target = sep_index + 1
        partner = blocks[target // per_device][target % per_device]
        spec_row = sky_spectrum[0, sep_index]
        scaled = (spec_row[None, None, :] * beam_matrix[0].astype(jnp.float32)).astype(jnp.bfloat16)
        right = jnp.concatenate([partner[0], partner[1]], axis=-1)
        top = jnp.concatenate([scaled[0], scaled[1]], axis=-1)
        bottom = jnp.concatenate([scaled[1], -scaled[0]], axis=-1)
        left = jnp.stack([top, bottom], axis=1).reshape(2 * mode_count, top.shape[-1])
        product = lax.dot_general(
            left, right, (((1,), (1,)), ((), ())), preferred_element_type=jnp.float32
        ).reshape(mode_count, 2, mode_count)
        term_list.append(
            lax.psum_scatter(
                product.astype(jnp.bfloat16), ("ell", "pol"), scatter_dimension=0, tiled=True
            ).astype(jnp.float32)
        )
    return jnp.stack(term_list)


T12, T13, T02, T03, TEND = range(5)


def meet_kernel(
    cut, own, spec, out,
    outer, near, far, spec0, spec1, stage, inbox, back_out, back_in, final_out, final_in,
    spec_s, spec_r, near_s, near_r, o1_s, o1_r, o2_s, o2_r, fw_s, fw_r,
    rs_s, rs_r, bk_s, bk_r, fn_s, fn_r,
):
    f32, bf16 = jnp.float32, jnp.bfloat16
    _, groups, rows, width = own.shape
    modes = groups * rows
    chunks = CHUNKS
    step = rows // chunks
    freqs = lax.axis_size("freq")
    pols = lax.axis_size("pol")
    freq = lax.axis_index("freq")
    me = lax.axis_index("ell") * pols + lax.axis_index("pol")
    low, high, full = (0, cut), (cut, width), (0, width)
    every = slice(None)

    barrier = pltpu.get_barrier_semaphore()
    for d in range(1, freqs):
        pl.semaphore_signal(
            barrier, inc=1, device_id={"freq": lax.rem(freq + d, freqs)},
            device_id_type=pl.DeviceIdType.MESH,
        )
    for d in range(1, groups):
        other = lax.rem(me + d, groups)
        pl.semaphore_signal(
            barrier, inc=1, device_id={"ell": other // pols, "pol": lax.rem(other, pols)},
            device_id_type=pl.DeviceIdType.MESH,
        )
    pl.semaphore_wait(barrier, freqs - 1 + groups - 1)

    def span(c):
        return pl.ds(pl.multiple_of(c * step, step), step)

    def to_freq(src, dst, send, recv, target):
        return pltpu.make_async_remote_copy(
            src_ref=src, dst_ref=dst, send_sem=send, recv_sem=recv,
            device_id={"freq": target}, device_id_type=pl.DeviceIdType.MESH,
        )

    def lanes(part):
        return pl.ds(part[0], part[1] - part[0])

    def send_spec(n, src, dst, target):
        return to_freq(src, dst, spec_s.at[n], spec_r.at[n], target)

    def mid(part, target):
        where = (every, every, every, lanes(part))
        return to_freq(own.at[where], near.at[where], near_s.at[0], near_r.at[0], target)

    def row_chunk(c, part):
        return (every, every, span(c), lanes(part))

    def block_chunk(g, part):
        return (every, pl.ds(g, 1), every, lanes(part))

    def hop(src, dst, send, recv, c, where, target):
        return to_freq(src.at[where], dst.at[where], send.at[c], recv.at[c], target)

    def share(tile, piece, where):
        copies = []
        for d in range(1, groups):
            other = lax.rem(me + d, groups)
            copies.append(
                pltpu.make_async_remote_copy(
                    src_ref=stage.at[(tile, other) + where],
                    dst_ref=inbox.at[(tile, d - 1) + where],
                    send_sem=rs_s.at[tile, piece, d - 1],
                    recv_sem=rs_r.at[tile, piece, d - 1],
                    device_id={"ell": other // pols, "pol": lax.rem(other, pols)},
                    device_id_type=pl.DeviceIdType.MESH,
                )
            )
        return copies

    def start_share(tile, piece, where):
        for copy in share(tile, piece, where):
            copy.start()

    whole = (every, every, every)

    def rows_of(c):
        return (every, span(c), every)

    def cols_of(g):
        return (every, every, pl.ds(pl.multiple_of(g * rows, rows), rows))

    def dot(a, b):
        return lax.dot_general(a, b, (((1,), (1,)), ((), ())), preferred_element_type=f32)

    def scaled(block, part_index, where, weight):
        value = block[(part_index,) + where].reshape(-1, weight.shape[-1])
        return (weight * value.astype(f32)).astype(bf16)

    def cross(left, left_where, weight, right, right_where):
        a_re = scaled(left, 0, left_where, weight)
        a_im = scaled(left, 1, left_where, weight)
        b_re = right[(0,) + right_where].reshape(-1, weight.shape[-1])
        b_im = right[(1,) + right_where].reshape(-1, weight.shape[-1])
        real = dot(a_re, b_re) + dot(a_im, b_im)
        imag = dot(a_im, b_re) - dot(a_re, b_im)
        return real.astype(bf16), imag.astype(bf16)

    def by_rows(tile, c, left, weights, sep, right, part):
        weight = weights[pl.ds(sep, 1), lanes(part)]
        real, imag = cross(
            left, (every, span(c), lanes(part)), weight, right, (every, every, lanes(part))
        )
        stage[tile, :, 0, span(c), :] = real.reshape(groups, step, modes)
        stage[tile, :, 1, span(c), :] = imag.reshape(groups, step, modes)

    def by_columns(tile, g, left, weights, sep, right, part):
        weight = weights[pl.ds(sep, 1), lanes(part)]
        columns = pl.ds(pl.multiple_of(g * rows, rows), rows)

        def body(o, carry):
            real, imag = cross(
                left, (o, every, lanes(part)), weight, right, (g, every, lanes(part))
            )
            stage[tile, o, 0, :, columns] = real
            stage[tile, o, 1, :, columns] = imag
            return carry

        lax.fori_loop(0, groups, body, 0)

    def gathered(tile, piece, where):
        for copy in share(tile, piece, where):
            copy.wait_recv()
        total = stage[(tile, me) + where].astype(f32)
        for d in range(groups - 1):
            total = total + inbox[(tile, d) + where].astype(f32)
        return total

    def loop(lo, hi, body):
        def wrapped(i, carry):
            body(i)
            return carry

        lax.fori_loop(lo, hi, wrapped, 0)

    def settle(tile, pieces, where_of):
        def body(c):
            for copy in share(tile, c, where_of(c)):
                copy.wait_send()

        loop(0, pieces, body)

    def give_back(tile, c, where):
        return to_freq(
            back_out.at[(tile,) + where], back_in.at[(tile,) + where],
            bk_s.at[tile, c], bk_r.at[tile, c], 0 if tile in (T02, T03) else 1,
        )

    def deliver(sep, c):
        where = rows_of(c)
        return to_freq(
            final_out.at[(sep,) + where], final_in.at[(sep,) + where],
            fn_s.at[sep, c], fn_r.at[sep, c], 0,
        )

    @pl.when(freq == 0)
    def _():
        send_spec(0, spec, spec0, 1).start()
        send_spec(1, spec, spec0, 2).start()
        loop(0, chunks, lambda c: hop(own, outer, o1_s, o1_r, c, row_chunk(c, high), 1).start())
        loop(0, chunks, lambda c: hop(own, outer, o2_s, o2_r, c, row_chunk(c, low), 1).start())
        send_spec(0, spec, spec0, 1).wait_send()
        send_spec(1, spec, spec0, 2).wait_send()
        loop(0, chunks, lambda c: hop(own, outer, o1_s, o1_r, c, row_chunk(c, high), 1).wait_send())
        loop(0, chunks, lambda c: hop(own, outer, o2_s, o2_r, c, row_chunk(c, low), 1).wait_send())

        def land(c):
            for sep, tile in ((1, T02), (2, T03)):
                where = rows_of(c)
                deliver(sep, c).wait_recv()
                give_back(tile, c, where).wait_recv()
                total = final_in[(sep,) + where].astype(f32) + back_in[(tile,) + where].astype(f32)
                out[(sep,) + where] = total.astype(bf16)

        loop(0, chunks, lambda c: deliver(0, c).wait_recv())
        out[0] = final_in[0]
        loop(0, chunks, land)

    @pl.when(freq == 3)
    def _():
        loop(0, groups, lambda g: hop(own, outer, o1_s, o1_r, g, block_chunk(g, low), 2).start())
        loop(0, groups, lambda g: hop(own, outer, o2_s, o2_r, g, block_chunk(g, high), 2).start())
        out[...] = jnp.zeros_like(out)
        loop(0, groups, lambda g: hop(own, outer, o1_s, o1_r, g, block_chunk(g, low), 2).wait_send())
        loop(0, groups, lambda g: hop(own, outer, o2_s, o2_r, g, block_chunk(g, high), 2).wait_send())

    @pl.when(freq == 1)
    def _():
        send_spec(2, spec, spec1, 2).start()
        mid(high, 2).start()

        def relay(c):
            hop(own, outer, o1_s, o1_r, c, row_chunk(c, high), 1).wait_recv()
            hop(outer, far, fw_s, fw_r, c, row_chunk(c, high), 2).start()

        loop(0, chunks - 1, relay)
        mid(low, 1).wait_recv()
        loop(0, chunks, lambda c: by_rows(T12, c, own, spec, 0, near, low))
        start_share(T12, 0, whole)
        loop(chunks - 1, chunks, relay)
        send_spec(0, spec, spec0, 1).wait_recv()

        def finish_end(c):
            final_out[(0,) + rows_of(c)] = gathered(TEND, c, rows_of(c)).astype(bf16)
            deliver(0, c).start()

        def cross_end(tile, sep):
            def body(c):
                where = rows_of(c)
                final_out[(sep,) + where] = gathered(tile, c, where).astype(bf16)
                deliver(sep, c).start()

            return body

        def block_in(g):
            hop(outer, far, fw_s, fw_r, g, block_chunk(g, low), 1).wait_recv()

        def columns_end(g):
            by_columns(T13, g, own, spec, 1, far, low)
            start_share(T13, g, cols_of(g))

        def near_end(g):
            block_in(g)
            columns_end(g)

        def take(c):
            hop(own, outer, o2_s, o2_r, c, row_chunk(c, low), 1).wait_recv()
            by_rows(TEND, c, outer, spec0, 0, own, full)
            start_share(TEND, c, rows_of(c))
            by_rows(T02, c, outer, spec0, 1, near, low)
            start_share(T02, c, rows_of(c))

            def last(r):
                by_rows(T03, r, outer, spec0, 2, far, low)
                start_share(T03, r, rows_of(r))

            first = jnp.where(c == chunks - 2, 0, c)
            stop = jnp.where(c >= chunks - 2, c + 1, 0)
            loop(c, jnp.where(c < chunks - 2, c + 1, c), near_end)
            loop(chunks - 2, jnp.where(c == chunks - 2, chunks, 0), block_in)
            loop(first, stop, last)
            before = jnp.maximum(c - 1, 0)
            loop(before, c, finish_end)
            loop(before, c, cross_end(T02, 1))
            loop(0, jnp.where(c == chunks - 1, c, 0), cross_end(T03, 2))

        loop(0, chunks, take)
        loop(chunks - 2, chunks, columns_end)
        loop(chunks - 1, chunks, finish_end)

        loop(chunks - 1, chunks, cross_end(T02, 1))
        loop(chunks - 1, chunks, cross_end(T03, 2))
        out[2] = jnp.zeros(out.shape[1:], bf16)
        give_back(T12, 0, whole).wait_recv()
        total = gathered(T12, 0, whole) + back_in[T12].astype(f32)
        out[0] = total.astype(bf16)
        give_back(T13, 0, whole).wait_recv()

        def own_columns(g):
            where = cols_of(g)
            total = gathered(T13, g, where) + back_in[(T13,) + where].astype(f32)
            out[(1,) + where] = total.astype(bf16)

        loop(0, groups, own_columns)

        send_spec(2, spec, spec1, 2).wait_send()
        mid(high, 2).wait_send()
        loop(0, chunks, lambda c: hop(outer, far, fw_s, fw_r, c, row_chunk(c, high), 2).wait_send())
        for tile, pieces, where_of in (
            (T12, 1, lambda c: whole), (T13, groups, cols_of),
            (T02, chunks, rows_of), (T03, chunks, rows_of), (TEND, chunks, rows_of),
        ):
            settle(tile, pieces, where_of)
        for sep in range(3):
            loop(0, chunks, lambda c: deliver(sep, c).wait_send())

    @pl.when(freq == 2)
    def _():
        mid(low, 1).start()

        def relay(g):
            hop(own, outer, o1_s, o1_r, g, block_chunk(g, low), 2).wait_recv()
            hop(outer, far, fw_s, fw_r, g, block_chunk(g, low), 1).start()

        loop(0, groups, relay)
        send_spec(1, spec, spec0, 2).wait_recv()
        send_spec(2, spec, spec1, 2).wait_recv()
        mid(high, 2).wait_recv()
        loop(0, chunks, lambda c: by_rows(T12, c, near, spec1, 0, own, high))
        start_share(T12, 0, whole)

        def return_rows(tile):
            def body(c):
                where = rows_of(c)
                back_out[(tile,) + where] = gathered(tile, c, where).astype(bf16)
                give_back(tile, c, where).start()

            return body

        def row_product(tile, sep, right):
            def body(c):
                by_rows(tile, c, far, spec0, sep, right, high)
                start_share(tile, c, rows_of(c))

            return body

        def end_product(g):
            by_columns(TEND, g, own, spec, 0, outer, full)
            start_share(TEND, g, cols_of(g))

        def take_columns(g):
            hop(own, outer, o2_s, o2_r, g, block_chunk(g, high), 2).wait_recv()
            by_columns(T13, g, near, spec1, 1, outer, high)
            start_share(T13, g, cols_of(g))
            loop(g, jnp.minimum(g + 1, groups - 1), end_product)

        per = chunks // groups
        late = chunks - per

        def take(c):
            due = jnp.where(lax.rem(c, per) == 0, 1, 0)
            loop(c // per, c // per + due, take_columns)

            @pl.when(c == 0)
            def _():
                back_out[T12] = gathered(T12, 0, whole).astype(bf16)
                give_back(T12, 0, whole).start()

            @pl.when(c == late)
            def _():
                loop(0, late, row_product(T03, 2, outer))
                loop(0, groups, return_columns)
                give_back(T13, 0, whole).start()

            hop(outer, far, fw_s, fw_r, c, row_chunk(c, high), 2).wait_recv()
            row_product(T02, 1, own)(c)
            loop(c, jnp.where(c >= late, c + 1, c), row_product(T03, 2, outer))
            loop(jnp.maximum(c - 1, 0), c, return_rows(T02))
            loop(jnp.where(c == late, 0, jnp.maximum(c - 1, 0)), jnp.where(c >= late, c, 0), return_rows(T03))

        def return_columns(g):
            where = cols_of(g)
            back_out[(T13,) + where] = gathered(T13, g, where).astype(bf16)

        loop(0, chunks, take)
        loop(groups - 1, groups, end_product)
        loop(chunks - 1, chunks, return_rows(T02))
        loop(chunks - 1, chunks, return_rows(T03))

        def end_columns(g):
            where = cols_of(g)
            out[(0,) + where] = gathered(TEND, g, where).astype(bf16)

        loop(0, groups, end_columns)
        out[1] = jnp.zeros(out.shape[1:], bf16)
        out[2] = jnp.zeros(out.shape[1:], bf16)

        mid(low, 1).wait_send()
        loop(0, groups, lambda g: hop(outer, far, fw_s, fw_r, g, block_chunk(g, low), 1).wait_send())
        for tile, pieces, where_of in (
            (T12, 1, lambda c: whole), (T13, groups, cols_of),
            (T02, chunks, rows_of), (T03, chunks, rows_of), (TEND, groups, cols_of),
        ):
            settle(tile, pieces, where_of)
        give_back(T12, 0, whole).wait_send()
        give_back(T13, 0, whole).wait_send()
        loop(0, chunks, lambda c: give_back(T02, c, rows_of(c)).wait_send())
        loop(0, chunks, lambda c: give_back(T03, c, rows_of(c)).wait_send())


def meet_sums(beam_matrix, sky_spectrum, local_rows):
    _, parts, modes, width = beam_matrix.shape
    separations = sky_spectrum.shape[1]
    groups = modes // local_rows
    tiles = 4 * 2 * local_rows * modes
    block = parts * modes * width
    cut = int(width * (0.5 - tiles / (4 * block))) // LANES * LANES
    pieces = max(CHUNKS, groups)
    bf16 = jnp.bfloat16
    shape = (parts, groups, local_rows, width)
    tile = (2, local_rows, modes)
    dma = pltpu.SemaphoreType.DMA
    pair = lambda *dims: [dma(dims), dma(dims)]
    return pl.pallas_call(
        functools.partial(meet_kernel, cut),
        out_shape=jax.ShapeDtypeStruct((separations,) + tile, bf16),
        in_specs=[pl.BlockSpec(memory_space=pltpu.VMEM)] * 2,
        out_specs=pl.BlockSpec(memory_space=pltpu.VMEM),
        scratch_shapes=[
            pltpu.VMEM(shape, bf16),
            pltpu.VMEM(shape, bf16),
            pltpu.VMEM(shape, bf16),
            pltpu.VMEM(sky_spectrum.shape[1:], jnp.float32),
            pltpu.VMEM(sky_spectrum.shape[1:], jnp.float32),
            pltpu.VMEM((5, groups) + tile, bf16),
            pltpu.VMEM((5, groups - 1) + tile, bf16),
            pltpu.VMEM((4,) + tile, bf16),
            pltpu.VMEM((4,) + tile, bf16),
            pltpu.VMEM((3,) + tile, bf16),
            pltpu.VMEM((3,) + tile, bf16),
            *pair(3), *pair(1), *pair(pieces), *pair(pieces), *pair(pieces),
            *pair(5, pieces, groups - 1), *pair(4, pieces), *pair(3, pieces),
        ],
        compiler_params=pltpu.CompilerParams(
            collective_id=0, has_side_effects=True, vmem_limit_bytes=60 * 2**20
        ),
    )(beam_matrix[0].reshape(shape), sky_spectrum[0])


def local(beam_matrix, sky_spectrum, taper_tiles, noise_tiles):
    per_device, _, modes, width = beam_matrix.shape
    separations = sky_spectrum.shape[1]
    local_rows = taper_tiles.shape[1]
    in_line = (
        per_device == 1
        and separations == 3
        and lax.axis_size("freq") == separations + 1
        and modes // local_rows == CHUNKS
        and local_rows % LANES == 0
        and width % (8 * LANES) == 0
    )
    if in_line:
        summed = meet_sums(beam_matrix, sky_spectrum, local_rows)
        summed = jnp.swapaxes(summed, 1, 2).astype(jnp.float32)
    else:
        summed = general_sums(beam_matrix, sky_spectrum, local_rows)
    summed = summed.reshape(per_device, separations, local_rows, 2, modes)
    taper = taper_tiles.astype(jnp.float32)[None, :, :, None, :]
    return taper * summed + noise_tiles.astype(jnp.float32)


def solution(mesh):
    placed = (
        P(("grp", "freq"), None, None, ("ell", "pol")),
        P(("grp", "freq"), None, ("ell", "pol")),
        P(None, ("ell", "pol"), None),
        P(("grp", "freq"), None, ("ell", "pol"), None, None),
    )
    return jax.shard_map(
        local,
        mesh=mesh,
        in_specs=placed,
        out_specs=P(("grp", "freq"), None, ("ell", "pol"), None, None),
        check_vma=False,
    )
```

profile of v0, /device:TPU:0, one launch (start us, length us, event | category | flops | bytes accessed | tf_op | source)
XLA Modules:
  0.0 136.5 jit_solution(1136774264788361176)
XLA Ops:
  0.0 1.4 copy.10
  1.4 0.0 copy-start.2
  1.4 0.0 copy-start.1
  1.4 131.3 %shard_map.46 = bf16[3,2,128,512]{3,2,1,0:T(8,128)(2,1)} custom-call(bf16[2,4,128,2048]{3,2,1,0:T(8,128)(2,1)} %bitcast.8, f32[3,2048]{1,0:T(4,128)} %bitcast.9), custom_call_target="tpu_custom_call" | custom-call | tf_op jit(solution)/shard_map/pallas_call | solution.py:441
  132.7 0.0 copy-done.2
  132.7 0.0 copy-start
  132.7 0.1 convert_element_type.10
  132.8 0.0 copy-done.1
  132.8 1.0 copy-done
  133.9 0.3 bitcast_add_fusion
  134.2 2.4 %copy.6 = f32[1,3,128,2,512]{4,3,2,1,0:T(2,128)} copy(f32[1,3,128,2,512]{4,2,3,1,0:T(8,128)S(1)} %bitcast_add_fusion) | data formatting | bytes 3145728 | tf_op jit(solution)/shard_map/add | solution.py:486
Async XLA Ops:
  1.4 131.3 %copy-start.2 = (bf16[3,128,512]{2,1,0:T(8,128)(2,1)S(1)}, bf16[3,128,512]{2,1,0:T(8,128)(2,1)}, u32[]{:S(2)}) copy-start(bf16[3,128,512]{2,1,0:T(8,128)(2,1)} %param.6) | copy-start | bytes 1179652
  1.4 131.5 %copy-start.1 = (bf16[1,3,128,2,512]{4,3,2,1,0:T(2,128)(2,1)S(1)}, bf16[1,3,128,2,512]{4,3,2,1,0:T(2,128)(2,1)}, u32[]{:S(2)}) copy-start(bf16[1,3,128,2,512]{4,3,2,1,0:T(2,128)(2,1)} %param.7) | copy-start | bytes 2359300
  132.7 1.1 copy-start
where the time goes:
time: 137 us
  Pallas kernels  131 us (96%)
  local copies, waits for them, and re-layouts  4.76 us (3%)
    pallas_call x1, Pallas kernels, meet_sums(): pl.pallas_call(functools.partial(meet_kernel, cut), out_shape=jax.ShapeDt...  131 us

commit v1 on v0

v1 whole, which is shorter than its diff:
```python
import functools

import jax
import jax.numpy as jnp
from jax import lax
from jax.experimental import pallas as pl
from jax.experimental.pallas import tpu as pltpu
from jax.sharding import PartitionSpec as P

FINE = 8
COARSE = 4
LATE = 2
LANES = 128


def passed_along(block, axis, distance):
    devices = range(lax.axis_size(axis))
    route = [(i - distance, i) for i in devices if i - distance in devices]
    return lax.ppermute(block, axis, route)


def general_sums(beam_matrix, sky_spectrum, local_rows):
    per_device = beam_matrix.shape[0]
    mode_count = beam_matrix.shape[2]
    separations = sky_spectrum.shape[1]
    needed = (per_device - 1 + separations) // per_device
    blocks = [beam_matrix]
    for offset in range(needed):
        blocks.append(passed_along(beam_matrix, "freq", -(offset + 1)))
    term_list = []
    for sep_index in range(separations):
        target = sep_index + 1
        partner = blocks[target // per_device][target % per_device]
        spec_row = sky_spectrum[0, sep_index]
        scaled = (spec_row[None, None, :] * beam_matrix[0].astype(jnp.float32)).astype(jnp.bfloat16)
        right = jnp.concatenate([partner[0], partner[1]], axis=-1)
        top = jnp.concatenate([scaled[0], scaled[1]], axis=-1)
        bottom = jnp.concatenate([scaled[1], -scaled[0]], axis=-1)
        left = jnp.stack([top, bottom], axis=1).reshape(2 * mode_count, top.shape[-1])
        product = lax.dot_general(
            left, right, (((1,), (1,)), ((), ())), preferred_element_type=jnp.float32
        ).reshape(mode_count, 2, mode_count)
        term_list.append(
            lax.psum_scatter(
                product.astype(jnp.bfloat16), ("ell", "pol"), scatter_dimension=0, tiled=True
            ).astype(jnp.float32)
        )
    return jnp.stack(term_list)


S0, S1, S2, S3 = range(4)


def meet_kernel(
    cut, own_hbm, spec, taper, out,
    own, outer, near, far, spec0, spec1, stage, inbox, back_out, back_in, final_out, final_in,
    load, spec_s, spec_r, hi_s, hi_r, lo_s, lo_r, mid_s, mid_r, nr_s, nr_r, fr_s, fr_r, fl_s, fl_r,
    rs_s, rs_r, bk_s, bk_r, fn_s, fn_r,
):
    f32, bf16 = jnp.float32, jnp.bfloat16
    _, groups, rows, width = own.shape
    modes = groups * rows
    fine, coarse, halves = FINE, COARSE, 2
    few = fine - LATE
    freqs = lax.axis_size("freq")
    pols = lax.axis_size("pol")
    freq = lax.axis_index("freq")
    me = lax.axis_index("ell") * pols + lax.axis_index("pol")
    low, high, full = (0, cut), (cut, width), (0, width)
    every = slice(None)
    per_row = 2 * modes // LANES

    loading = pltpu.make_async_copy(own_hbm, own, load)
    loading.start()

    barrier = pltpu.get_barrier_semaphore()
    for d in range(1, freqs):
        pl.semaphore_signal(
            barrier, inc=1, device_id={"freq": lax.rem(freq + d, freqs)},
            device_id_type=pl.DeviceIdType.MESH,
        )
    for d in range(1, groups):
        other = lax.rem(me + d, groups)
        pl.semaphore_signal(
            barrier, inc=1, device_id={"ell": other // pols, "pol": lax.rem(other, pols)},
            device_id_type=pl.DeviceIdType.MESH,
        )
    pl.semaphore_wait(barrier, freqs - 1 + groups - 1)

    def span(c, pieces):
        step = rows // pieces
        return pl.ds(pl.multiple_of(c * step, step), step)

    def to_freq(src, dst, send, recv, target):
        return pltpu.make_async_remote_copy(
            src_ref=src, dst_ref=dst, send_sem=send, recv_sem=recv,
            device_id={"freq": target}, device_id_type=pl.DeviceIdType.MESH,
        )

    def lanes(part):
        return pl.ds(part[0], part[1] - part[0])

    def loop(lo, hi, body):
        def wrapped(i, carry):
            body(i)
            return carry

        lax.fori_loop(lo, hi, wrapped, 0)

    def send_spec(dst, n, target):
        which = 0 if dst is spec0 else 1
        return to_freq(spec, dst, spec_s.at[n], spec_r.at[which], target)

    def moved(src, dst, where, send, recv, target):
        return to_freq(src.at[where], dst.at[where], send, recv, target)

    def row_piece(c, pieces, part):
        return (every, every, span(c, pieces), lanes(part))

    def block_piece(g, count, part):
        return (every, pl.ds(g * count, count), every, lanes(part))

    def outer_high(c):
        return moved(own_hbm, outer, row_piece(c, fine, high), hi_s.at[c], hi_r.at[c], 1)

    def outer_low(c):
        return moved(own_hbm, outer, row_piece(c, coarse, low), lo_s.at[c], lo_r.at[c], 1)

    def first_on(src, c, target):
        return moved(src, near, row_piece(c, fine, high), nr_s.at[c], nr_r.at[c], target)

    def second_on(src, c, target):
        return moved(src, far, row_piece(c, fine, high), fr_s.at[c], fr_r.at[c], target)

    def last_low(g):
        return moved(own_hbm, outer, block_piece(g, 1, low), lo_s.at[g], lo_r.at[g], 2)

    def last_high(g):
        return moved(
            own_hbm, outer, block_piece(g, groups // halves, high), hi_s.at[g], hi_r.at[g], 2
        )

    def last_on(g):
        return moved(outer, far, block_piece(g, 1, low), fl_s.at[g], fl_r.at[g], 1)

    def third_on(src, g, target):
        return moved(src, near, block_piece(g, 1, low), mid_s.at[g], mid_r.at[g], target)

    def share(slot, piece, where):
        copies = []
        for d in range(1, groups):
            other = lax.rem(me + d, groups)
            copies.append(
                pltpu.make_async_remote_copy(
                    src_ref=stage.at[(slot, other) + where],
                    dst_ref=inbox.at[(slot, d - 1) + where],
                    send_sem=rs_s.at[slot, piece, d - 1],
                    recv_sem=rs_r.at[slot, piece, d - 1],
                    device_id={"ell": other // pols, "pol": lax.rem(other, pols)},
                    device_id_type=pl.DeviceIdType.MESH,
                )
            )
        return copies

    def start_share(slot, piece, where):
        for copy in share(slot, piece, where):
            copy.start()

    def rows_of(c, pieces):
        return (every, span(c, pieces), every)

    def cols_of(g):
        size = modes // halves
        return (every, every, pl.ds(pl.multiple_of(g * size, size), size))

    def dot(a, b):
        return lax.dot_general(a, b, (((1,), (1,)), ((), ())), preferred_element_type=f32)

    def cross(left, left_where, weight, right, right_where):
        def scaled(part_index):
            value = left[(part_index,) + left_where].reshape(-1, weight.shape[-1])
            return (weight * value.astype(f32)).astype(bf16)

        a_re, a_im = scaled(0), scaled(1)
        b_re = right[(0,) + right_where].reshape(-1, weight.shape[-1])
        b_im = right[(1,) + right_where].reshape(-1, weight.shape[-1])
        both = dot(jnp.concatenate([a_re, a_im], 0), b_re)
        both = both + dot(jnp.concatenate([a_im, -a_re], 0), b_im)
        size = a_re.shape[0]
        return both[:size].astype(bf16), both[size:].astype(bf16)

    def by_rows(slot, c, pieces, left, weights, sep, right, part):
        weight = weights[sep, :, lanes(part)]
        real, imag = cross(
            left, (every, span(c, pieces), lanes(part)), weight, right, (every, every, lanes(part))
        )
        stage[slot, :, 0, span(c, pieces), :] = real.reshape(groups, rows // pieces, modes)
        stage[slot, :, 1, span(c, pieces), :] = imag.reshape(groups, rows // pieces, modes)
        start_share(slot, c, rows_of(c, pieces))

    def by_columns(slot, g, left, weights, sep, right, part):
        weight = weights[sep, :, lanes(part)]
        count = groups // halves
        columns = cols_of(g)[-1]

        def body(o):
            real, imag = cross(
                left, (o, every, lanes(part)), weight,
                right, (pl.ds(g * count, count), every, lanes(part)),
            )
            stage[slot, o, 0, :, columns] = real
            stage[slot, o, 1, :, columns] = imag

        loop(0, groups, body)
        start_share(slot, g, cols_of(g))

    def await_share(slot, piece, where):
        for copy in share(slot, piece, where):
            copy.wait_recv()

    def added(slot, where):
        total = stage[(slot, me) + where].astype(f32)
        for d in range(groups - 1):
            total = total + inbox[(slot, d) + where].astype(f32)
        return total

    def settle(slot, pieces, where_of, lo=0):
        def body(c):
            for copy in share(slot, c, where_of(c)):
                copy.wait_send()

        loop(lo, pieces, body)

    def fine_rows(c):
        return rows_of(c, fine)

    def coarse_rows(c):
        return rows_of(c, coarse)

    def give_back(slot, c):
        where = fine_rows(c)
        return to_freq(
            back_out.at[(slot,) + where], back_in.at[(slot,) + where],
            bk_s.at[slot, c], bk_r.at[slot, c], 0 if slot in (S0, S3) else 1,
        )

    def returned(slot):
        def body(c):
            where = fine_rows(c)
            await_share(slot, c, where)
            back_out[(slot,) + where] = added(slot, where).astype(bf16)
            give_back(slot, c).start()

        return body

    def deliver(n, c):
        where = coarse_rows(c)
        return to_freq(
            final_out.at[(n,) + where], final_in.at[(n,) + where], fn_s.at[n, c], fn_r.at[n, c], 0
        )

    def delivered(slot, n):
        def body(c):
            where = coarse_rows(c)
            await_share(slot, c, where)
            final_out[(n,) + where] = added(slot, where).astype(bf16)
            deliver(n, c).start()

        return body

    def finish(sep, first_row, count, first_block, total):
        weight = taper[sep, pl.ds(first_row, count), pl.ds(first_block * LANES, total.shape[-1])]
        weight = weight.astype(f32)
        for part in range(2):
            value = weight * total[part]
            for j in range(total.shape[-1] // LANES):
                start = first_row * per_row + 2 * (first_block + j) + part
                out[sep, pl.ds(start, count, stride=per_row), :] = value[
                    :, j * LANES:(j + 1) * LANES
                ]

    def finish_rows(sep, c, pieces, total):
        step = rows // pieces
        finish(sep, pl.multiple_of(c * step, step), step, 0, total)

    def clear(sep):
        out[sep] = jnp.zeros(out.shape[1:], f32)

    @pl.when(freq == 0)
    def _():
        for n in range(1, freqs):
            send_spec(spec0, n - 1, n).start()
        loop(0, fine, lambda c: outer_high(c).start())
        loop(0, coarse, lambda c: outer_low(c).start())
        loading.wait()
        loop(0, groups, lambda g: third_on(near, g, 0).wait_recv())
        loop(0, coarse, lambda c: by_rows(S0, c, coarse, own, spec, 1, near, low))
        loop(0, coarse, lambda c: await_share(S0, c, coarse_rows(c)))

        def ends(c):
            deliver(0, c).wait_recv()
            finish_rows(0, c, coarse, final_in[(0,) + coarse_rows(c)].astype(f32))

        def middles(c):
            where = fine_rows(c)
            give_back(S0, c).wait_recv()
            finish_rows(1, c, fine, added(S0, where) + back_in[(S0,) + where].astype(f32))

        def longs(c):
            per = fine // coarse
            where = fine_rows(c)

            @pl.when(lax.rem(c, per) == 0)
            def _():
                deliver(1, c // per).wait_recv()

            give_back(S3, c).wait_recv()
            total = final_in[(1,) + where].astype(f32) + back_in[(S3,) + where].astype(f32)
            finish_rows(2, c, fine, total)

        loop(0, coarse - 1, ends)
        loop(0, fine, middles)
        loop(coarse - 1, coarse, ends)
        loop(0, fine, longs)
        for n in range(1, freqs):
            send_spec(spec0, n - 1, n).wait_send()
        loop(0, fine, lambda c: outer_high(c).wait_send())
        loop(0, coarse, lambda c: outer_low(c).wait_send())
        settle(S0, coarse, coarse_rows)

    @pl.when(freq == 1)
    def _():
        for n in range(2):
            second_on(own_hbm, n, 2).start()
            send_spec(spec1, n, n + 2).start()
        clear(2)

        def relay(c):
            outer_high(c).wait_recv()
            first_on(outer, c, 2).start()

        def relay_back(g):
            third_on(own_hbm, g, 1).wait_recv()
            third_on(near, g, 0).start()

        done = 0
        for c in range(fine):
            relay(c)
            while done < groups and 2 * fine * (done + 1) <= groups * (2 * c + 3):
                relay_back(done)
                done += 1
        for g in range(done, groups):
            relay_back(g)
        loop(2, fine, lambda c: second_on(own_hbm, c, 2).start())
        loading.wait()
        send_spec(spec0, 0, 1).wait_recv()
        loop(0, coarse, lambda c: by_rows(S1, c, coarse, own, spec, 0, near, low))

        def take(c):
            outer_low(c).wait_recv()
            by_rows(S0, c, coarse, outer, spec0, 0, own, full)

            @pl.when(c == coarse - 2)
            def _():
                loop(0, groups, lambda g: last_on(g).wait_recv())
                loop(0, coarse, lambda r: by_rows(S2, r, coarse, own, spec, 1, far, low))

            @pl.when(c >= coarse - 2)
            def _():
                loop(
                    jnp.where(c == coarse - 2, 0, c), c + 1,
                    lambda r: by_rows(S3, r, coarse, outer, spec0, 2, far, low),
                )

            loop(jnp.maximum(c - 1, 0), c, delivered(S0, 0))
            loop(0, jnp.where(c == coarse - 1, c, 0), delivered(S3, 1))

        loop(0, coarse, take)
        loop(coarse - 1, coarse, delivered(S0, 0))
        loop(coarse - 1, coarse, delivered(S3, 1))
        loop(0, coarse, lambda c: await_share(S1, c, coarse_rows(c)))
        loop(0, coarse, lambda c: await_share(S2, c, coarse_rows(c)))

        def ends(slot, sep):
            def body(c):
                where = fine_rows(c)
                give_back(slot, c).wait_recv()
                finish_rows(sep, c, fine, added(slot, where) + back_in[(slot,) + where].astype(f32))

            return body

        loop(0, few, ends(S1, 0))
        loop(0, few, ends(S2, 1))

        def late(c):
            ends(S1, 0)(c)
            ends(S2, 1)(c)

        loop(few, fine, late)
        for n in range(2):
            send_spec(spec1, n, n + 2).wait_send()
        loop(0, fine, lambda c: second_on(own_hbm, c, 2).wait_send())
        loop(0, fine, lambda c: first_on(outer, c, 2).wait_send())
        loop(0, groups, lambda g: third_on(near, g, 0).wait_send())
        for slot in range(4):
            settle(slot, coarse, coarse_rows)
        for n in range(2):
            loop(0, coarse, lambda c: deliver(n, c).wait_send())

    @pl.when(freq == 2)
    def _():
        loop(0, groups, lambda g: third_on(own_hbm, g, 1).start())
        clear(1)
        clear(2)
        loading.wait()
        send_spec(spec0, 1, 2).wait_recv()
        send_spec(spec1, 0, 2).wait_recv()

        def second(c):
            second_on(own_hbm, c, 2).wait_recv()
            second_on(far, c, 3).start()
            by_rows(S1, c, fine, far, spec1, 0, own, high)

        def first(c):
            first_on(outer, c, 2).wait_recv()
            first_on(near, c, 3).start()

            @pl.when(c < groups)
            def _():
                last_low(c).wait_recv()
                last_on(c).start()

            by_rows(S0, c, fine, near, spec0, 1, own, high)
            loop(jnp.maximum(c - 1, 0), c, returned(S0))

        def block(g):
            last_high(g).wait_recv()
            by_columns(S3, g, own, spec, 0, outer, full)

        loop(0, 2, second)
        loop(0, 1, returned(S1))
        loop(0, fine, first)
        loop(1, 2, returned(S1))

        def second_more(c):
            second(c)
            loop(c - 1, jnp.where(c > 2, c, c - 1), returned(S1))
            loop(fine - 1, jnp.where(c == 2, fine, fine - 1), returned(S0))
            loop(0, jnp.where(c == 2, 1, 0), block)

        loop(2, few, second_more)
        loop(few - 1, few, returned(S1))
        loop(1, halves, block)

        def tail(c):
            second_on(own_hbm, c, 2).wait_recv()
            by_rows(S1, c, fine, far, spec1, 0, own, high)
            by_rows(S2, c, fine, far, spec1, 1, outer, high)
            returned(S1)(c)
            returned(S2)(c)

        loop(few, fine, tail)
        for g in range(halves):
            where = cols_of(g)
            await_share(S3, g, where)
            size = modes // halves
            finish(0, 0, rows, g * size // LANES, added(S3, where))

        loop(0, groups, lambda g: third_on(own_hbm, g, 1).wait_send())
        loop(0, groups, lambda g: last_on(g).wait_send())
        loop(0, fine, lambda c: first_on(near, c, 3).wait_send())
        loop(0, few, lambda c: second_on(far, c, 3).wait_send())
        settle(S0, fine, fine_rows)
        settle(S1, fine, fine_rows)
        settle(S2, fine, fine_rows, few)
        settle(S3, halves, cols_of)
        loop(0, fine, lambda c: give_back(S0, c).wait_send())
        loop(0, fine, lambda c: give_back(S1, c).wait_send())
        loop(few, fine, lambda c: give_back(S2, c).wait_send())

    @pl.when(freq == 3)
    def _():
        loop(0, groups, lambda g: last_low(g).start())
        loop(0, halves, lambda g: last_high(g).start())
        for sep in range(3):
            clear(sep)
        loading.wait()
        send_spec(spec0, 2, 3).wait_recv()
        send_spec(spec1, 1, 3).wait_recv()

        def second(c):
            second_on(far, c, 3).wait_recv()
            by_rows(S2, c, fine, far, spec1, 1, own, high)
            returned(S2)(c)

        def first(c):
            first_on(near, c, 3).wait_recv()
            by_rows(S3, c, fine, near, spec0, 2, own, high)
            returned(S3)(c)

        loop(0, 2, second)
        loop(0, fine, first)
        loop(2, few, second)
        loop(0, groups, lambda g: last_low(g).wait_send())
        loop(0, halves, lambda g: last_high(g).wait_send())
        settle(S3, fine, fine_rows)
        settle(S2, few, fine_rows)
        loop(0, fine, lambda c: give_back(S3, c).wait_send())
        loop(0, few, lambda c: give_back(S2, c).wait_send())


def meet_covariance(beam_matrix, sky_spectrum, taper_tiles):
    _, parts, modes, width = beam_matrix.shape
    separations, local_rows, _ = taper_tiles.shape
    groups = modes // local_rows
    tiles = 4 * 2 * local_rows * modes
    block = parts * modes * width
    cut = int(width * (0.5 - tiles / (4 * block))) // LANES * LANES
    bf16, f32 = jnp.bfloat16, jnp.float32
    shape = (parts, groups, local_rows, width)
    tile = (2, local_rows, modes)
    blocks = modes // LANES
    dma = pltpu.SemaphoreType.DMA
    pair = lambda *dims: [dma(dims), dma(dims)]
    vmem = pl.BlockSpec(memory_space=pltpu.VMEM)
    spec = jnp.swapaxes(sky_spectrum, 0, 1)
    lines = pl.pallas_call(
        functools.partial(meet_kernel, cut),
        out_shape=jax.ShapeDtypeStruct((separations, local_rows * blocks * 2, LANES), f32),
        in_specs=[pl.BlockSpec(memory_space=pl.ANY), vmem, vmem],
        out_specs=vmem,
        scratch_shapes=[
            *[pltpu.VMEM(shape, bf16)] * 4,
            *[pltpu.VMEM(spec.shape, f32)] * 2,
            pltpu.VMEM((4, groups) + tile, bf16),
            pltpu.VMEM((4, groups - 1) + tile, bf16),
            *[pltpu.VMEM((4,) + tile, bf16)] * 2,
            *[pltpu.VMEM((2,) + tile, bf16)] * 2,
            dma, *pair(3), *pair(FINE), *pair(max(COARSE, groups)), *pair(groups),
            *pair(FINE), *pair(FINE), *pair(groups),
            *pair(4, FINE, groups - 1), *pair(4, FINE), *pair(2, COARSE),
        ],
        compiler_params=pltpu.CompilerParams(
            collective_id=0, has_side_effects=True, vmem_limit_bytes=60 * 2**20
        ),
    )(beam_matrix[0].reshape(shape), spec, taper_tiles)
    lines = lines.reshape(1, separations, local_rows, blocks, 2, LANES)
    return jnp.swapaxes(lines, 3, 4).reshape(1, separations, local_rows, 2, modes)


def local(beam_matrix, sky_spectrum, taper_tiles, noise_tiles):
    per_device, _, modes, width = beam_matrix.shape
    separations = sky_spectrum.shape[1]
    local_rows = taper_tiles.shape[1]
    in_line = (
        per_device == 1
        and separations == 3
        and lax.axis_size("freq") == separations + 1
        and modes // local_rows == 4
        and local_rows % LANES == 0
        and width % (8 * LANES) == 0
    )
    noise = noise_tiles.astype(jnp.float32)
    if in_line:
        return meet_covariance(beam_matrix, sky_spectrum, taper_tiles) + noise
    summed = general_sums(beam_matrix, sky_spectrum, local_rows)
    summed = summed.reshape(per_device, separations, local_rows, 2, modes)
    taper = taper_tiles.astype(jnp.float32)[None, :, :, None, :]
    return taper * summed + noise


def solution(mesh):
    placed = (
        P(("grp", "freq"), None, None, ("ell", "pol")),
        P(("grp", "freq"), None, ("ell", "pol")),
        P(None, ("ell", "pol"), None),
        P(("grp", "freq"), None, ("ell", "pol"), None, None),
    )
    return jax.shard_map(
        local,
        mesh=mesh,
        in_specs=placed,
        out_specs=P(("grp", "freq"), None, ("ell", "pol"), None, None),
        check_vma=False,
    )
```

time: 137 us -> 131 us (0.956)
  the two profiles are of different devices: /device:TPU:0 before, /device:TPU:8 now
where the time goes in v1:
time: 131 us; the launch traced here: 130 us
  Pallas kernels  128 us (98%)
  other arithmetic  2.83 us (2%)
    pallas_call x1, Pallas kernels, meet_covariance(): pl.pallas_call(functools.partial(meet_kernel, cut), out_shape=jax.ShapeDt...  128 us
    add x1, other arithmetic, local(): return meet_covariance(beam_matrix, sky_spectrum, taper_tiles) + noise  2.83 us

profile of v1, /device:TPU:8, one launch (start us, length us, event | category | flops | bytes accessed | tf_op | source)
XLA Modules:
  0.0 130.5 jit_solution(11786130559806645975)
XLA Ops:
  0.0 0.0 copy-start
  0.0 127.6 %shard_map.46 = f32[3,1024,128]{2,1,0:T(8,128)} custom-call(bf16[2,4,128,2048]{3,2,1,0:T(8,128)(2,1)} %bitcast.11, f32[3,1,2048]{2,1,0:T(1,128)} %bitcast.13, bf16[3,128,512]{2,1,0:T(8,128)(2,1)} %taper.1), custom_call_target="tpu_custom_call" | custom-call | tf_op jit(solution)/shard_map/pallas_call | solution.py:527
  127.6 0.0 copy-done
  127.7 2.8 %convert_add_fusion = f32[1,3,32,8,512]{4,3,2,1,0:T(8,128)} fusion(f32[1,3,32,8,512]{4,3,2,1,0:T(8,128)} %bitcast.10, bf16[1,3,32,8,512]{4,3,2,1,0:T(8,128)(2,1)S(1)} %bitcast.12), kind=kLoop, calls=%fused_computation | loop fusion | flops 786432 | bytes 3932160 | tf_op jit(solution)/shard_map/add | solution.py:565
Async XLA Ops:
  0.0 127.6 %copy-start = (bf16[1,3,128,2,512]{4,3,2,1,0:T(2,128)(2,1)S(1)}, bf16[1,3,128,2,512]{4,3,2,1,0:T(2,128)(2,1)}, u32[]{:S(2)}) copy-start(bf16[1,3,128,2,512]{4,3,2,1,0:T(2,128)(2,1)} %param.7) | copy-start | bytes 2359300

commit v2 on v1

--- a/solution.py
+++ b/solution.py
@@ -52,15 +52,16 @@
 
 
 def meet_kernel(
-    cut, own_hbm, spec, taper, out,
-    own, outer, near, far, spec0, spec1, stage, inbox, back_out, back_in, final_out, final_in,
-    load, spec_s, spec_r, hi_s, hi_r, lo_s, lo_r, mid_s, mid_r, nr_s, nr_r, fr_s, fr_r, fl_s, fl_r,
+    cut, own_hbm, spec, taper_hbm, out,
+    own, taper, outer, near, far, spec0, spec1, stage, inbox, back_out, back_in, final_out, final_in,
+    load, load_taper, spec_s, spec_r, hi_s, hi_r, lo_s, lo_r, mid_s, mid_r, nr_s, nr_r, fr_s, fr_r, fl_s, fl_r,
     rs_s, rs_r, bk_s, bk_r, fn_s, fn_r,
 ):
     f32, bf16 = jnp.float32, jnp.bfloat16
     _, groups, rows, width = own.shape
     modes = groups * rows
     fine, coarse, halves = FINE, COARSE, 2
+    held = groups // halves
     few = fine - LATE
     freqs = lax.axis_size("freq")
     pols = lax.axis_size("pol")
@@ -72,6 +73,8 @@
 
     loading = pltpu.make_async_copy(own_hbm, own, load)
     loading.start()
+    tapers = pltpu.make_async_copy(taper_hbm, taper, load_taper)
+    tapers.start()
 
     barrier = pltpu.get_barrier_semaphore()
     for d in range(1, freqs):
@@ -107,9 +110,21 @@
 
         lax.fori_loop(lo, hi, wrapped, 0)
 
-    def send_spec(dst, n, target):
-        which = 0 if dst is spec0 else 1
-        return to_freq(spec, dst, spec_s.at[n], spec_r.at[which], target)
+    def send_spec(dst, sep, part, n, target):
+        where = (pl.ds(sep, 1), every, lanes(part))
+        return to_freq(spec.at[where], dst.at[where], spec_s.at[n], spec_r.at[n], target)
+
+    def own_first():
+        return [
+            send_spec(spec0, 0, full, 0, 1), send_spec(spec0, 1, high, 1, 2),
+            send_spec(spec0, 2, high, 2, 3), send_spec(spec0, 2, low, 3, 1),
+        ]
+
+    def own_second():
+        return [
+            send_spec(spec1, 0, high, 4, 2), send_spec(spec1, 1, high, 5, 3),
+            send_spec(spec1, 1, high, 6, 2),
+        ]
 
     def moved(src, dst, where, send, recv, target):
         return to_freq(src.at[where], dst.at[where], send, recv, target)
@@ -136,9 +151,7 @@
         return moved(own_hbm, outer, block_piece(g, 1, low), lo_s.at[g], lo_r.at[g], 2)
 
     def last_high(g):
-        return moved(
-            own_hbm, outer, block_piece(g, groups // halves, high), hi_s.at[g], hi_r.at[g], 2
-        )
+        return moved(own_hbm, outer, block_piece(g, 1, high), hi_s.at[g], hi_r.at[g], 2)
 
     def last_on(g):
         return moved(outer, far, block_piece(g, 1, low), fl_s.at[g], fl_r.at[g], 1)
@@ -169,9 +182,12 @@
     def rows_of(c, pieces):
         return (every, span(c, pieces), every)
 
-    def cols_of(g):
-        size = modes // halves
+    def cols_of(g, count=1):
+        size = count * rows
         return (every, every, pl.ds(pl.multiple_of(g * size, size), size))
+
+    def wide_cols(g):
+        return cols_of(g, held)
 
     def dot(a, b):
         return lax.dot_general(a, b, (((1,), (1,)), ((), ())), preferred_element_type=f32)
@@ -198,10 +214,9 @@
         stage[slot, :, 1, span(c, pieces), :] = imag.reshape(groups, rows // pieces, modes)
         start_share(slot, c, rows_of(c, pieces))
 
-    def by_columns(slot, g, left, weights, sep, right, part):
+    def by_columns(slot, g, count, left, weights, sep, right, part):
         weight = weights[sep, :, lanes(part)]
-        count = groups // halves
-        columns = cols_of(g)[-1]
+        columns = cols_of(g, count)[-1]
 
         def body(o):
             real, imag = cross(
@@ -212,7 +227,7 @@
             stage[slot, o, 1, :, columns] = imag
 
         loop(0, groups, body)
-        start_share(slot, g, cols_of(g))
+        start_share(slot, g, cols_of(g, count))
 
     def await_share(slot, piece, where):
         for copy in share(slot, piece, where):
@@ -288,11 +303,13 @@
 
     @pl.when(freq == 0)
     def _():
-        for n in range(1, freqs):
-            send_spec(spec0, n - 1, n).start()
-        loop(0, fine, lambda c: outer_high(c).start())
+        outer_high(0).start()
+        for copy in own_first():
+            copy.start()
+        loop(1, fine, lambda c: outer_high(c).start())
         loop(0, coarse, lambda c: outer_low(c).start())
         loading.wait()
+        tapers.wait()
         loop(0, groups, lambda g: third_on(near, g, 0).wait_recv())
         loop(0, coarse, lambda c: by_rows(S0, c, coarse, own, spec, 1, near, low))
         loop(0, coarse, lambda c: await_share(S0, c, coarse_rows(c)))
@@ -322,17 +339,18 @@
         loop(0, fine, middles)
         loop(coarse - 1, coarse, ends)
         loop(0, fine, longs)
-        for n in range(1, freqs):
-            send_spec(spec0, n - 1, n).wait_send()
+        for copy in own_first():
+            copy.wait_send()
         loop(0, fine, lambda c: outer_high(c).wait_send())
         loop(0, coarse, lambda c: outer_low(c).wait_send())
         settle(S0, coarse, coarse_rows)
 
     @pl.when(freq == 1)
     def _():
-        for n in range(2):
-            second_on(own_hbm, n, 2).start()
-            send_spec(spec1, n, n + 2).start()
+        second_on(own_hbm, 0, 2).start()
+        for copy in own_second():
+            copy.start()
+        second_on(own_hbm, 1, 2).start()
         clear(2)
 
         def relay(c):
@@ -353,17 +371,23 @@
             relay_back(g)
         loop(2, fine, lambda c: second_on(own_hbm, c, 2).start())
         loading.wait()
-        send_spec(spec0, 0, 1).wait_recv()
+        tapers.wait()
+        own_first()[0].wait_recv()
+        own_first()[3].wait_recv()
         loop(0, coarse, lambda c: by_rows(S1, c, coarse, own, spec, 0, near, low))
 
         def take(c):
             outer_low(c).wait_recv()
             by_rows(S0, c, coarse, outer, spec0, 0, own, full)
 
+            @pl.when(c == 0)
+            def _():
+                loop(0, held, lambda g: last_on(g).wait_recv())
+                by_columns(S2, 0, held, own, spec, 1, far, low)
+
             @pl.when(c == coarse - 2)
             def _():
-                loop(0, groups, lambda g: last_on(g).wait_recv())
-                loop(0, coarse, lambda r: by_rows(S2, r, coarse, own, spec, 1, far, low))
+                loop(held, groups, lambda g: last_on(g).wait_recv())
 
             @pl.when(c >= coarse - 2)
             def _():
@@ -376,10 +400,10 @@
             loop(0, jnp.where(c == coarse - 1, c, 0), delivered(S3, 1))
 
         loop(0, coarse, take)
+        loop(1, halves, lambda g: by_columns(S2, g, held, own, spec, 1, far, low))
         loop(coarse - 1, coarse, delivered(S0, 0))
         loop(coarse - 1, coarse, delivered(S3, 1))
         loop(0, coarse, lambda c: await_share(S1, c, coarse_rows(c)))
-        loop(0, coarse, lambda c: await_share(S2, c, coarse_rows(c)))
 
         def ends(slot, sep):
             def body(c):
@@ -390,6 +414,7 @@
             return body
 
         loop(0, few, ends(S1, 0))
+        loop(0, halves, lambda g: await_share(S2, g, wide_cols(g)))
         loop(0, few, ends(S2, 1))
 
         def late(c):
@@ -397,13 +422,14 @@
             ends(S2, 1)(c)
 
         loop(few, fine, late)
-        for n in range(2):
-            send_spec(spec1, n, n + 2).wait_send()
+        for copy in own_second():
+            copy.wait_send()
         loop(0, fine, lambda c: second_on(own_hbm, c, 2).wait_send())
         loop(0, fine, lambda c: first_on(outer, c, 2).wait_send())
         loop(0, groups, lambda g: third_on(near, g, 0).wait_send())
-        for slot in range(4):
+        for slot in (S0, S1, S3):
             settle(slot, coarse, coarse_rows)
+        settle(S2, halves, wide_cols)
         for n in range(2):
             loop(0, coarse, lambda c: deliver(n, c).wait_send())
 
@@ -413,8 +439,8 @@
         clear(1)
         clear(2)
         loading.wait()
-        send_spec(spec0, 1, 2).wait_recv()
-        send_spec(spec1, 0, 2).wait_recv()
+        tapers.wait()
+        own_second()[0].wait_recv()
 
         def second(c):
             second_on(own_hbm, c, 2).wait_recv()
@@ -431,40 +457,48 @@
                 last_on(c).start()
 
             by_rows(S0, c, fine, near, spec0, 1, own, high)
-            loop(jnp.maximum(c - 1, 0), c, returned(S0))
+            loop(0, jnp.where(c == groups, 2, 0), returned(S1))
+            before = jnp.where(c == groups, 0, jnp.maximum(c - 1, 0))
+            loop(before, jnp.where(c >= groups, c, before), returned(S0))
 
         def block(g):
+            by_columns(S3, g, 1, own, spec, 0, outer, full)
+
+        def block_in(g):
             last_high(g).wait_recv()
-            by_columns(S3, g, own, spec, 0, outer, full)
 
         loop(0, 2, second)
-        loop(0, 1, returned(S1))
+        own_first()[1].wait_recv()
+        own_second()[2].wait_recv()
         loop(0, fine, first)
-        loop(1, 2, returned(S1))
 
         def second_more(c):
             second(c)
             loop(c - 1, jnp.where(c > 2, c, c - 1), returned(S1))
             loop(fine - 1, jnp.where(c == 2, fine, fine - 1), returned(S0))
-            loop(0, jnp.where(c == 2, 1, 0), block)
+            g = jnp.where(c < few - 1, c - 2, groups - 2)
+            stop = jnp.where(c < 2 + groups - 2, g + 1, jnp.where(c == few - 1, groups - 1, g))
+            loop(g, stop, block_in)
+            loop(g, stop, block)
 
         loop(2, few, second_more)
         loop(few - 1, few, returned(S1))
-        loop(1, halves, block)
 
         def tail(c):
             second_on(own_hbm, c, 2).wait_recv()
             by_rows(S1, c, fine, far, spec1, 0, own, high)
+            last = jnp.where(c == few, groups, groups - 1)
+            loop(groups - 1, last, block_in)
             by_rows(S2, c, fine, far, spec1, 1, outer, high)
+            loop(groups - 1, last, block)
             returned(S1)(c)
             returned(S2)(c)
 
         loop(few, fine, tail)
-        for g in range(halves):
+        for g in range(groups):
             where = cols_of(g)
             await_share(S3, g, where)
-            size = modes // halves
-            finish(0, 0, rows, g * size // LANES, added(S3, where))
+            finish(0, 0, rows, g * rows // LANES, added(S3, where))
 
         loop(0, groups, lambda g: third_on(own_hbm, g, 1).wait_send())
         loop(0, groups, lambda g: last_on(g).wait_send())
@@ -473,7 +507,7 @@
         settle(S0, fine, fine_rows)
         settle(S1, fine, fine_rows)
         settle(S2, fine, fine_rows, few)
-        settle(S3, halves, cols_of)
+        settle(S3, groups, cols_of)
         loop(0, fine, lambda c: give_back(S0, c).wait_send())
         loop(0, fine, lambda c: give_back(S1, c).wait_send())
         loop(few, fine, lambda c: give_back(S2, c).wait_send())
@@ -481,12 +515,11 @@
     @pl.when(freq == 3)
     def _():
         loop(0, groups, lambda g: last_low(g).start())
-        loop(0, halves, lambda g: last_high(g).start())
         for sep in range(3):
             clear(sep)
         loading.wait()
-        send_spec(spec0, 2, 3).wait_recv()
-        send_spec(spec1, 1, 3).wait_recv()
+        tapers.wait()
+        own_second()[1].wait_recv()
 
         def second(c):
             second_on(far, c, 3).wait_recv()
@@ -497,12 +530,15 @@
             first_on(near, c, 3).wait_recv()
             by_rows(S3, c, fine, near, spec0, 2, own, high)
             returned(S3)(c)
+            loop(held, jnp.where(c == fine // 2, groups, held), lambda g: last_high(g).start())
 
         loop(0, 2, second)
+        loop(0, held, lambda g: last_high(g).start())
+        own_first()[2].wait_recv()
         loop(0, fine, first)
         loop(2, few, second)
         loop(0, groups, lambda g: last_low(g).wait_send())
-        loop(0, halves, lambda g: last_high(g).wait_send())
+        loop(0, groups, lambda g: last_high(g).wait_send())
         settle(S3, fine, fine_rows)
         settle(S2, few, fine_rows)
         loop(0, fine, lambda c: give_back(S3, c).wait_send())
@@ -523,25 +559,27 @@
     dma = pltpu.SemaphoreType.DMA
     pair = lambda *dims: [dma(dims), dma(dims)]
     vmem = pl.BlockSpec(memory_space=pltpu.VMEM)
+    hbm = pl.BlockSpec(memory_space=pltpu.HBM)
     spec = jnp.swapaxes(sky_spectrum, 0, 1)
     lines = pl.pallas_call(
         functools.partial(meet_kernel, cut),
         out_shape=jax.ShapeDtypeStruct((separations, local_rows * blocks * 2, LANES), f32),
-        in_specs=[pl.BlockSpec(memory_space=pl.ANY), vmem, vmem],
+        in_specs=[hbm, vmem, hbm],
         out_specs=vmem,
         scratch_shapes=[
-            *[pltpu.VMEM(shape, bf16)] * 4,
+            pltpu.VMEM(shape, bf16), pltpu.VMEM(taper_tiles.shape, bf16),
+            *[pltpu.VMEM(shape, bf16)] * 3,
             *[pltpu.VMEM(spec.shape, f32)] * 2,
             pltpu.VMEM((4, groups) + tile, bf16),
             pltpu.VMEM((4, groups - 1) + tile, bf16),
             *[pltpu.VMEM((4,) + tile, bf16)] * 2,
             *[pltpu.VMEM((2,) + tile, bf16)] * 2,
-            dma, *pair(3), *pair(FINE), *pair(max(COARSE, groups)), *pair(groups),
+            dma, dma, *pair(7), *pair(FINE), *pair(max(COARSE, groups)), *pair(groups),
             *pair(FINE), *pair(FINE), *pair(groups),
             *pair(4, FINE, groups - 1), *pair(4, FINE), *pair(2, COARSE),
         ],
         compiler_params=pltpu.CompilerParams(
-            collective_id=0, has_side_effects=True, vmem_limit_bytes=60 * 2**20
+            collective_id=0, has_side_effects=True, vmem_limit_bytes=51 * 2**20
         ),
     )(beam_matrix[0].reshape(shape), spec, taper_tiles)
     lines = lines.reshape(1, separations, local_rows, blocks, 2, LANES)

time: 131 us -> 122 us (0.931)
  Pallas kernels: 128 us -> 119 us
  local copies, waits for them, and re-layouts: 0.01 us -> 1.74 us
  other arithmetic: 2.83 us -> 1.38 us
    pallas_call x1, Pallas kernels: 128 us -> 119 us  [meet_covariance(): pl.pallas_call(functools.partial(meet_kernel, cut), out_shape=jax.ShapeDt...]
    unnamed x2 -> x6, local copies, waits for them, and re-layouts: 0.01 us -> 1.74 us
    add x1, other arithmetic: 2.83 us -> 1.38 us  [local(): return meet_covariance(beam_matrix, sky_spectrum, taper_tiles) + noise]
where the time goes in v2:
time: 122 us
  Pallas kernels  119 us (98%)
  local copies, waits for them, and re-layouts  1.74 us (1%)
  other arithmetic  1.38 us (1%)
    pallas_call x1, Pallas kernels, meet_covariance(): pl.pallas_call(functools.partial(meet_kernel, cut), out_shape=jax.ShapeDt...  119 us

profile of v2, /device:TPU:8, one launch (start us, length us, event | category | flops | bytes accessed | tf_op | source)
XLA Modules:
  0.0 122.0 jit_solution(4761138887740835596)
XLA Ops:
  0.0 0.0 copy-start
  0.0 1.0 copy-done
  1.0 0.0 copy-start.1
  1.0 0.7 copy-done.1
  1.7 0.0 copy-start.2
  1.7 118.9 %shard_map.46 = f32[3,1024,128]{2,1,0:T(8,128)S(1)} custom-call(bf16[2,4,128,2048]{3,2,1,0:T(8,128)(2,1)} %bitcast.12, f32[3,1,2048]{2,1,0:T(1,128)S(1)} %bitcast.11, bf16[3,128,512]{2,1,0:T(8,128)(2,1)S(1)} %copy-done), custom_call_target="tpu_custom_call" | custom-call | tf_op jit(solution)/shard_map/pallas_call | solution.py:564
  120.6 0.0 copy-done.2
  120.7 1.4 %convert_add_fusion = f32[1,3,32,8,512]{4,3,2,1,0:T(8,128)} fusion(f32[1,3,32,8,512]{4,3,2,1,0:T(8,128)S(1)} %bitcast.10, bf16[1,3,32,8,512]{4,3,2,1,0:T(8,128)(2,1)S(1)} %bitcast.13), kind=kLoop, calls=%fused_computation | loop fusion | flops 786432 | bytes 3932160 | tf_op jit(solution)/shard_map/add | solution.py:603
Async XLA Ops:
  0.0 1.0 copy-start
  1.0 0.7 copy-start.1
  1.7 118.9 %copy-start.2 = (bf16[1,3,128,2,512]{4,3,2,1,0:T(2,128)(2,1)S(1)}, bf16[1,3,128,2,512]{4,3,2,1,0:T(2,128)(2,1)}, u32[]{:S(2)}) copy-start(bf16[1,3,128,2,512]{4,3,2,1,0:T(2,128)(2,1)} %param.7) | copy-start | bytes 2359300

commit v3 on v2

--- a/solution.py
+++ b/solution.py
@@ -9,7 +9,9 @@
 
 FINE = 8
 COARSE = 4
+LEAD = 2
 LATE = 2
+EDGE = 2
 LANES = 128
 
 
@@ -52,9 +54,9 @@
 
 
 def meet_kernel(
-    cut, own_hbm, spec, taper_hbm, out,
-    own, taper, outer, near, far, spec0, spec1, stage, inbox, back_out, back_in, final_out, final_in,
-    load, load_taper, spec_s, spec_r, hi_s, hi_r, lo_s, lo_r, mid_s, mid_r, nr_s, nr_r, fr_s, fr_r, fl_s, fl_r,
+    cut, own_hbm, spec_hbm, taper_hbm, out,
+    own, spec, taper, outer, near, far, spec0, spec1, stage, inbox, back_out, back_in, final_out, final_in, held_sum,
+    load, load_spec, load_taper, spec_s, spec_r, hi_s, hi_r, lo_s, lo_r, mid_s, mid_r, nr_s, nr_r, fr_s, fr_r, fl_s, fl_r,
     rs_s, rs_r, bk_s, bk_r, fn_s, fn_r,
 ):
     f32, bf16 = jnp.float32, jnp.bfloat16
@@ -63,32 +65,46 @@
     fine, coarse, halves = FINE, COARSE, 2
     held = groups // halves
     few = fine - LATE
+    gap = fine // (groups + 1)
+    settled = gap * (groups - 1) + 1
     freqs = lax.axis_size("freq")
     pols = lax.axis_size("pol")
     freq = lax.axis_index("freq")
     me = lax.axis_index("ell") * pols + lax.axis_index("pol")
     low, high, full = (0, cut), (cut, width), (0, width)
+    edge = width - EDGE * LANES
+    lasts = ((cut, edge), (edge, width))
     every = slice(None)
     per_row = 2 * modes // LANES
 
     loading = pltpu.make_async_copy(own_hbm, own, load)
     loading.start()
+    spectra = pltpu.make_async_copy(spec_hbm, spec, load_spec)
+    spectra.start()
     tapers = pltpu.make_async_copy(taper_hbm, taper, load_taper)
     tapers.start()
 
     barrier = pltpu.get_barrier_semaphore()
-    for d in range(1, freqs):
+    @pl.when(freq > 0)
+    def _():
         pl.semaphore_signal(
-            barrier, inc=1, device_id={"freq": lax.rem(freq + d, freqs)},
-            device_id_type=pl.DeviceIdType.MESH,
-        )
+            barrier, inc=1, device_id={"freq": freq - 1}, device_id_type=pl.DeviceIdType.MESH
+        )
+
+    @pl.when(freq < freqs - 1)
+    def _():
+        pl.semaphore_signal(
+            barrier, inc=1, device_id={"freq": freq + 1}, device_id_type=pl.DeviceIdType.MESH
+        )
+
     for d in range(1, groups):
         other = lax.rem(me + d, groups)
         pl.semaphore_signal(
             barrier, inc=1, device_id={"ell": other // pols, "pol": lax.rem(other, pols)},
             device_id_type=pl.DeviceIdType.MESH,
         )
-    pl.semaphore_wait(barrier, freqs - 1 + groups - 1)
+    beside = jnp.where(freq > 0, 1, 0) + jnp.where(freq < freqs - 1, 1, 0)
+    pl.semaphore_wait(barrier, beside + groups - 1)
 
     def span(c, pieces):
         step = rows // pieces
@@ -110,21 +126,19 @@
 
         lax.fori_loop(lo, hi, wrapped, 0)
 
-    def send_spec(dst, sep, part, n, target):
-        where = (pl.ds(sep, 1), every, lanes(part))
-        return to_freq(spec.at[where], dst.at[where], spec_s.at[n], spec_r.at[n], target)
-
-    def own_first():
-        return [
-            send_spec(spec0, 0, full, 0, 1), send_spec(spec0, 1, high, 1, 2),
-            send_spec(spec0, 2, high, 2, 3), send_spec(spec0, 2, low, 3, 1),
-        ]
-
-    def own_second():
-        return [
-            send_spec(spec1, 0, high, 4, 2), send_spec(spec1, 1, high, 5, 3),
-            send_spec(spec1, 1, high, 6, 2),
-        ]
+    def send_spec(src, dst, seps, part, n, target):
+        where = (pl.ds(seps[0], len(seps)), every, lanes(part))
+        return to_freq(src.at[where], dst.at[where], spec_s.at[n], spec_r.at[n], target)
+
+    def first_rows(target):
+        if target == 1:
+            return send_spec(spec_hbm, spec0, (0, 1, 2), full, 0, 1)
+        return send_spec(spec0, spec0, (1, 2) if target == 2 else (2,), high, target - 1, target)
+
+    def second_rows(target):
+        if target == 2:
+            return send_spec(spec_hbm, spec1, (0, 1), high, 3, 2)
+        return send_spec(spec1, spec1, (1,), high, 4, 3)
 
     def moved(src, dst, where, send, recv, target):
         return to_freq(src.at[where], dst.at[where], send, recv, target)
@@ -146,6 +160,11 @@
 
     def second_on(src, c, target):
         return moved(src, far, row_piece(c, fine, high), fr_s.at[c], fr_r.at[c], target)
+
+    def second_last(n):
+        where = row_piece(fine - 1, fine, lasts[n])
+        m = fine - 1 + n
+        return moved(own_hbm, far, where, fr_s.at[m], fr_r.at[m], 2)
 
     def last_low(g):
         return moved(own_hbm, outer, block_piece(g, 1, low), lo_s.at[g], lo_r.at[g], 2)
@@ -192,7 +211,7 @@
     def dot(a, b):
         return lax.dot_general(a, b, (((1,), (1,)), ((), ())), preferred_element_type=f32)
 
-    def cross(left, left_where, weight, right, right_where):
+    def product(left, left_where, weight, right, right_where):
         def scaled(part_index):
             value = left[(part_index,) + left_where].reshape(-1, weight.shape[-1])
             return (weight * value.astype(f32)).astype(bf16)
@@ -201,15 +220,23 @@
         b_re = right[(0,) + right_where].reshape(-1, weight.shape[-1])
         b_im = right[(1,) + right_where].reshape(-1, weight.shape[-1])
         both = dot(jnp.concatenate([a_re, a_im], 0), b_re)
-        both = both + dot(jnp.concatenate([a_im, -a_re], 0), b_im)
-        size = a_re.shape[0]
+        return both + dot(jnp.concatenate([a_im, -a_re], 0), b_im)
+
+    def cross(*operands):
+        both = product(*operands)
+        size = both.shape[0] // 2
         return both[:size].astype(bf16), both[size:].astype(bf16)
 
-    def by_rows(slot, c, pieces, left, weights, sep, right, part):
-        weight = weights[sep, :, lanes(part)]
-        real, imag = cross(
-            left, (every, span(c, pieces), lanes(part)), weight, right, (every, every, lanes(part))
-        )
+    def row_operands(c, pieces, left, weights, sep, right, part):
+        return (
+            left, (every, span(c, pieces), lanes(part)), weights[sep, :, lanes(part)],
+            right, (every, every, lanes(part)),
+        )
+
+    def by_rows(slot, c, pieces, *rest):
+        put_rows(slot, c, pieces, *cross(*row_operands(c, pieces, *rest)))
+
+    def put_rows(slot, c, pieces, real, imag):
         stage[slot, :, 0, span(c, pieces), :] = real.reshape(groups, rows // pieces, modes)
         stage[slot, :, 1, span(c, pieces), :] = imag.reshape(groups, rows // pieces, modes)
         start_share(slot, c, rows_of(c, pieces))
@@ -304,11 +331,11 @@
     @pl.when(freq == 0)
     def _():
         outer_high(0).start()
-        for copy in own_first():
-            copy.start()
+        first_rows(1).start()
         loop(1, fine, lambda c: outer_high(c).start())
         loop(0, coarse, lambda c: outer_low(c).start())
         loading.wait()
+        spectra.wait()
         tapers.wait()
         loop(0, groups, lambda g: third_on(near, g, 0).wait_recv())
         loop(0, coarse, lambda c: by_rows(S0, c, coarse, own, spec, 1, near, low))
@@ -339,8 +366,7 @@
         loop(0, fine, middles)
         loop(coarse - 1, coarse, ends)
         loop(0, fine, longs)
-        for copy in own_first():
-            copy.wait_send()
+        first_rows(1).wait_send()
         loop(0, fine, lambda c: outer_high(c).wait_send())
         loop(0, coarse, lambda c: outer_low(c).wait_send())
         settle(S0, coarse, coarse_rows)
@@ -348,9 +374,10 @@
     @pl.when(freq == 1)
     def _():
         second_on(own_hbm, 0, 2).start()
-        for copy in own_second():
-            copy.start()
-        second_on(own_hbm, 1, 2).start()
+        second_rows(2).start()
+        loop(1, LEAD, lambda c: second_on(own_hbm, c, 2).start())
+        first_rows(1).wait_recv()
+        first_rows(2).start()
         clear(2)
 
         def relay(c):
@@ -369,11 +396,12 @@
                 done += 1
         for g in range(done, groups):
             relay_back(g)
-        loop(2, fine, lambda c: second_on(own_hbm, c, 2).start())
+        loop(LEAD, fine - 1, lambda c: second_on(own_hbm, c, 2).start())
+        for n in range(2):
+            second_last(n).start()
         loading.wait()
+        spectra.wait()
         tapers.wait()
-        own_first()[0].wait_recv()
-        own_first()[3].wait_recv()
         loop(0, coarse, lambda c: by_rows(S1, c, coarse, own, spec, 0, near, low))
 
         def take(c):
@@ -421,10 +449,11 @@
             ends(S1, 0)(c)
             ends(S2, 1)(c)
 
-        loop(few, fine, late)
-        for copy in own_second():
-            copy.wait_send()
-        loop(0, fine, lambda c: second_on(own_hbm, c, 2).wait_send())
+        second_rows(2).wait_send()
+        first_rows(2).wait_send()
+        loop(0, fine - 1, lambda c: second_on(own_hbm, c, 2).wait_send())
+        for n in range(2):
+            second_last(n).wait_send()
         loop(0, fine, lambda c: first_on(outer, c, 2).wait_send())
         loop(0, groups, lambda g: third_on(near, g, 0).wait_send())
         for slot in (S0, S1, S3):
@@ -432,6 +461,7 @@
         settle(S2, halves, wide_cols)
         for n in range(2):
             loop(0, coarse, lambda c: deliver(n, c).wait_send())
+        loop(few, fine, late)
 
     @pl.when(freq == 2)
     def _():
@@ -439,8 +469,10 @@
         clear(1)
         clear(2)
         loading.wait()
+        spectra.wait()
         tapers.wait()
-        own_second()[0].wait_recv()
+        second_rows(2).wait_recv()
+        second_rows(3).start()
 
         def second(c):
             second_on(own_hbm, c, 2).wait_recv()
@@ -451,15 +483,17 @@
             first_on(outer, c, 2).wait_recv()
             first_on(near, c, 3).start()
 
-            @pl.when(c < groups)
+            g = c // gap
+
+            @pl.when(jnp.logical_and(lax.rem(c, gap) == 0, g < groups))
             def _():
-                last_low(c).wait_recv()
-                last_on(c).start()
+                last_low(g).wait_recv()
+                last_on(g).start()
 
             by_rows(S0, c, fine, near, spec0, 1, own, high)
-            loop(0, jnp.where(c == groups, 2, 0), returned(S1))
-            before = jnp.where(c == groups, 0, jnp.maximum(c - 1, 0))
-            loop(before, jnp.where(c >= groups, c, before), returned(S0))
+            loop(0, jnp.where(c == settled, LEAD, 0), returned(S1))
+            before = jnp.where(c == settled, 0, jnp.maximum(c - 1, 0))
+            loop(before, jnp.where(c >= settled, c, before), returned(S0))
 
         def block(g):
             by_columns(S3, g, 1, own, spec, 0, outer, full)
@@ -467,39 +501,52 @@
         def block_in(g):
             last_high(g).wait_recv()
 
-        loop(0, 2, second)
-        own_first()[1].wait_recv()
-        own_second()[2].wait_recv()
+        loop(0, LEAD, second)
+        first_rows(2).wait_recv()
+        first_rows(3).start()
         loop(0, fine, first)
 
         def second_more(c):
             second(c)
-            loop(c - 1, jnp.where(c > 2, c, c - 1), returned(S1))
-            loop(fine - 1, jnp.where(c == 2, fine, fine - 1), returned(S0))
-            g = jnp.where(c < few - 1, c - 2, groups - 2)
-            stop = jnp.where(c < 2 + groups - 2, g + 1, jnp.where(c == few - 1, groups - 1, g))
-            loop(g, stop, block_in)
-            loop(g, stop, block)
-
-        loop(2, few, second_more)
+            loop(c - 1, jnp.where(c > LEAD, c, c - 1), returned(S1))
+            loop(fine - 1, jnp.where(c == LEAD, fine, fine - 1), returned(S0))
+            g = jnp.where(c < LEAD + gap, 0, jnp.where(c < few - gap, 1, 2))
+            due = jnp.logical_or(c == LEAD, jnp.logical_or(c == LEAD + gap, c == few - gap))
+            loop(g, jnp.where(due, g + 1, g), block_in)
+            loop(g, jnp.where(due, g + 1, g), block)
+
+        loop(LEAD, few, second_more)
         loop(few - 1, few, returned(S1))
 
-        def tail(c):
+        def late(c):
             second_on(own_hbm, c, 2).wait_recv()
             by_rows(S1, c, fine, far, spec1, 0, own, high)
-            last = jnp.where(c == few, groups, groups - 1)
-            loop(groups - 1, last, block_in)
+            loop(groups - 1, jnp.where(c == few, groups, groups - 1), block_in)
             by_rows(S2, c, fine, far, spec1, 1, outer, high)
-            loop(groups - 1, last, block)
-            returned(S1)(c)
-            returned(S2)(c)
-
-        loop(few, fine, tail)
+            loop(groups - 1, jnp.where(c == few, groups, groups - 1), block)
+
+        loop(few, fine - 1, late)
+        c = fine - 1
+        ways = ((S1, own), (S2, outer))
+        second_last(0).wait_recv()
+        for n, (slot, right) in enumerate(ways):
+            held_sum[n] = product(*row_operands(c, fine, far, spec1, n, right, lasts[0]))
+        loop(few, c, returned(S1))
+        loop(few, c, returned(S2))
+        second_last(1).wait_recv()
+        for n, (slot, right) in enumerate(ways):
+            both = held_sum[n] + product(*row_operands(c, fine, far, spec1, n, right, lasts[1]))
+            size = both.shape[0] // 2
+            put_rows(slot, c, fine, both[:size].astype(bf16), both[size:].astype(bf16))
+        returned(S1)(c)
+        returned(S2)(c)
         for g in range(groups):
             where = cols_of(g)
             await_share(S3, g, where)
             finish(0, 0, rows, g * rows // LANES, added(S3, where))
 
+        second_rows(3).wait_send()
+        first_rows(3).wait_send()
         loop(0, groups, lambda g: third_on(own_hbm, g, 1).wait_send())
         loop(0, groups, lambda g: last_on(g).wait_send())
         loop(0, fine, lambda c: first_on(near, c, 3).wait_send())
@@ -518,8 +565,9 @@
         for sep in range(3):
             clear(sep)
         loading.wait()
+        spectra.wait()
         tapers.wait()
-        own_second()[1].wait_recv()
+        second_rows(3).wait_recv()
 
         def second(c):
             second_on(far, c, 3).wait_recv()
@@ -530,13 +578,13 @@
             first_on(near, c, 3).wait_recv()
             by_rows(S3, c, fine, near, spec0, 2, own, high)
             returned(S3)(c)
-            loop(held, jnp.where(c == fine // 2, groups, held), lambda g: last_high(g).start())
-
-        loop(0, 2, second)
+            loop(held, jnp.where(c == fine - groups, groups, held), lambda g: last_high(g).start())
+
+        loop(0, LEAD, second)
         loop(0, held, lambda g: last_high(g).start())
-        own_first()[2].wait_recv()
+        first_rows(3).wait_recv()
         loop(0, fine, first)
-        loop(2, few, second)
+        loop(LEAD, few, second)
         loop(0, groups, lambda g: last_low(g).wait_send())
         loop(0, groups, lambda g: last_high(g).wait_send())
         settle(S3, fine, fine_rows)
@@ -561,27 +609,30 @@
     vmem = pl.BlockSpec(memory_space=pltpu.VMEM)
     hbm = pl.BlockSpec(memory_space=pltpu.HBM)
     spec = jnp.swapaxes(sky_spectrum, 0, 1)
+    kept = lambda array: pltpu.with_memory_space_constraint(array, pltpu.HBM)
     lines = pl.pallas_call(
         functools.partial(meet_kernel, cut),
         out_shape=jax.ShapeDtypeStruct((separations, local_rows * blocks * 2, LANES), f32),
-        in_specs=[hbm, vmem, hbm],
+        in_specs=[hbm, hbm, hbm],
         out_specs=vmem,
         scratch_shapes=[
-            pltpu.VMEM(shape, bf16), pltpu.VMEM(taper_tiles.shape, bf16),
+            pltpu.VMEM(shape, bf16), pltpu.VMEM(spec.shape, f32),
+            pltpu.VMEM(taper_tiles.shape, bf16),
             *[pltpu.VMEM(shape, bf16)] * 3,
             *[pltpu.VMEM(spec.shape, f32)] * 2,
             pltpu.VMEM((4, groups) + tile, bf16),
             pltpu.VMEM((4, groups - 1) + tile, bf16),
             *[pltpu.VMEM((4,) + tile, bf16)] * 2,
             *[pltpu.VMEM((2,) + tile, bf16)] * 2,
-            dma, dma, *pair(7), *pair(FINE), *pair(max(COARSE, groups)), *pair(groups),
-            *pair(FINE), *pair(FINE), *pair(groups),
+            pltpu.VMEM((2, 2 * modes // FINE, modes), f32),
+            dma, dma, dma, *pair(5), *pair(FINE), *pair(max(COARSE, groups)), *pair(groups),
+            *pair(FINE), *pair(FINE + 1), *pair(groups),
             *pair(4, FINE, groups - 1), *pair(4, FINE), *pair(2, COARSE),
         ],
         compiler_params=pltpu.CompilerParams(
             collective_id=0, has_side_effects=True, vmem_limit_bytes=51 * 2**20
         ),
-    )(beam_matrix[0].reshape(shape), spec, taper_tiles)
+    )(kept(beam_matrix[0].reshape(shape)), kept(spec), kept(taper_tiles))
     lines = lines.reshape(1, separations, local_rows, blocks, 2, LANES)
     return jnp.swapaxes(lines, 3, 4).reshape(1, separations, local_rows, 2, modes)
 

time: 122 us -> 119 us (0.975)
  Pallas kernels: 119 us -> 117 us
  local copies, waits for them, and re-layouts: 1.74 us -> 0.01 us
    pallas_call x1, Pallas kernels: 119 us -> 117 us  [meet_covariance(): pl.pallas_call(functools.partial(meet_kernel, cut), out_shape=jax.ShapeDt...]
    unnamed x6 -> x2, local copies, waits for them, and re-layouts: 1.74 us -> 0.01 us
where the time goes in v3:
time: 119 us
  Pallas kernels  117 us (98%)
  other arithmetic  1.41 us (1%)
    pallas_call x1, Pallas kernels, meet_covariance(): pl.pallas_call(functools.partial(meet_kernel, cut), out_shape=jax.ShapeDt...  117 us

profile of v3, /device:TPU:8, one launch (start us, length us, event | category | flops | bytes accessed | tf_op | source)
XLA Modules:
  0.0 118.6 jit_solution(3268022333909052179)
XLA Ops:
  0.0 0.0 copy-start
  0.0 117.1 %shard_map.46 = f32[3,1024,128]{2,1,0:T(8,128)S(1)} custom-call(bf16[2,4,128,2048]{3,2,1,0:T(8,128)(2,1)} %bitcast.11, f32[3,1,2048]{2,1,0:T(1,128)} %bitcast.13, bf16[3,128,512]{2,1,0:T(8,128)(2,1)} %taper_hbm.1), custom_call_target="tpu_custom_call" | custom-call | tf_op jit(solution)/shard_map/pallas_call | solution.py:613
  117.1 0.0 copy-done
  117.2 1.4 %convert_add_fusion = f32[1,3,32,8,512]{4,3,2,1,0:T(8,128)} fusion(f32[1,3,32,8,512]{4,3,2,1,0:T(8,128)S(1)} %bitcast.10, bf16[1,3,32,8,512]{4,3,2,1,0:T(8,128)(2,1)S(1)} %bitcast.12), kind=kLoop, calls=%fused_computation | loop fusion | flops 786432 | bytes 3932160 | tf_op jit(solution)/shard_map/add | solution.py:654
Async XLA Ops:
  0.0 117.1 %copy-start = (bf16[1,3,128,2,512]{4,3,2,1,0:T(2,128)(2,1)S(1)}, bf16[1,3,128,2,512]{4,3,2,1,0:T(2,128)(2,1)}, u32[]{:S(2)}) copy-start(bf16[1,3,128,2,512]{4,3,2,1,0:T(2,128)(2,1)} %param.7) | copy-start | bytes 2359300

commit v4 on v3

--- a/solution.py
+++ b/solution.py
@@ -55,9 +55,9 @@
 
 def meet_kernel(
     cut, own_hbm, spec_hbm, taper_hbm, out,
-    own, spec, taper, outer, near, far, spec0, spec1, stage, inbox, back_out, back_in, final_out, final_in, held_sum,
+    own, spec, taper, outer, near, far, spec0, spec1, stage, inbox, back_out, back_in, final_out, final_in, held_sum, base, pair_out, pair_in,
     load, load_spec, load_taper, spec_s, spec_r, hi_s, hi_r, lo_s, lo_r, mid_s, mid_r, nr_s, nr_r, fr_s, fr_r, fl_s, fl_r,
-    rs_s, rs_r, bk_s, bk_r, fn_s, fn_r,
+    rs_s, rs_r, bk_s, bk_r, fn_s, fn_r, pair_s, pair_r,
 ):
     f32, bf16 = jnp.float32, jnp.bfloat16
     _, groups, rows, width = own.shape
@@ -70,7 +70,8 @@
     freqs = lax.axis_size("freq")
     pols = lax.axis_size("pol")
     freq = lax.axis_index("freq")
-    me = lax.axis_index("ell") * pols + lax.axis_index("pol")
+    line, core = lax.axis_index("ell"), lax.axis_index("pol")
+    me = line * pols + core
     low, high, full = (0, cut), (cut, width), (0, width)
     edge = width - EDGE * LANES
     lasts = ((cut, edge), (edge, width))
@@ -235,25 +236,30 @@
 
     def by_rows(slot, c, pieces, *rest):
         put_rows(slot, c, pieces, *cross(*row_operands(c, pieces, *rest)))
+        start_share(slot, c, rows_of(c, pieces))
 
     def put_rows(slot, c, pieces, real, imag):
         stage[slot, :, 0, span(c, pieces), :] = real.reshape(groups, rows // pieces, modes)
         stage[slot, :, 1, span(c, pieces), :] = imag.reshape(groups, rows // pieces, modes)
-        start_share(slot, c, rows_of(c, pieces))
-
-    def by_columns(slot, g, count, left, weights, sep, right, part):
-        weight = weights[sep, :, lanes(part)]
+
+    def column_product(o, g, count, left, weights, sep, right, part):
+        return product(
+            left, (pl.ds(o * held, held), every, lanes(part)), weights[sep, :, lanes(part)],
+            right, (pl.ds(g * count, count), every, lanes(part)),
+        )
+
+    def by_columns(slot, g, count, *operands, base=None):
         columns = cols_of(g, count)[-1]
 
         def body(o):
-            real, imag = cross(
-                left, (o, every, lanes(part)), weight,
-                right, (pl.ds(g * count, count), every, lanes(part)),
-            )
-            stage[slot, o, 0, :, columns] = real
-            stage[slot, o, 1, :, columns] = imag
-
-        loop(0, groups, body)
+            both = column_product(o, g, count, *operands)
+            both = both if base is None else both + base[o]
+            size = both.shape[0] // 2
+            real, imag = both[:size].astype(bf16), both[size:].astype(bf16)
+            stage[slot, pl.ds(o * held, held), 0, :, columns] = real.reshape(held, rows, -1)
+            stage[slot, pl.ds(o * held, held), 1, :, columns] = imag.reshape(held, rows, -1)
+
+        loop(0, halves, body)
         start_share(slot, g, cols_of(g, count))
 
     def await_share(slot, piece, where):
@@ -294,6 +300,36 @@
             give_back(slot, c).start()
 
         return body
+
+    def paired(slot):
+        where = fine_rows(fine - 1)
+        return [
+            pltpu.make_async_remote_copy(
+                src_ref=stage.at[(slot, e * pols + 1 - core) + where],
+                dst_ref=inbox.at[(slot, e) + where],
+                send_sem=rs_s.at[slot, fine - 1, e], recv_sem=rs_r.at[slot, fine - 1, e],
+                device_id={"pol": 1 - core}, device_id_type=pl.DeviceIdType.MESH,
+            )
+            for e in range(groups // pols)
+        ]
+
+    def pair_on(n, e, origin):
+        return pltpu.make_async_remote_copy(
+            src_ref=pair_out.at[n, e], dst_ref=pair_in.at[n, origin],
+            send_sem=pair_s.at[n, e], recv_sem=pair_r.at[n, origin],
+            device_id={"freq": 1, "ell": e}, device_id_type=pl.DeviceIdType.MESH,
+        )
+
+    def pairs_sent(n, slot):
+        where = fine_rows(fine - 1)
+        for copy in paired(slot):
+            copy.wait_recv()
+        for e in range(groups // pols):
+            total = stage[(slot, e * pols + core) + where].astype(f32)
+            total = total + inbox[(slot, e) + where].astype(f32)
+            pair_out[n, e] = total.astype(bf16)
+        pair_on(n, 1 - line, line).start()
+        pair_on(n, line, line).start()
 
     def deliver(n, c):
         where = coarse_rows(c)
@@ -461,7 +497,14 @@
         settle(S2, halves, wide_cols)
         for n in range(2):
             loop(0, coarse, lambda c: deliver(n, c).wait_send())
-        loop(few, fine, late)
+        loop(few, fine - 1, late)
+        where = fine_rows(fine - 1)
+        for n, slot in enumerate((S1, S2)):
+            total = added(slot, where)
+            for e in range(groups // pols):
+                pair_on(n, line, e).wait_recv()
+                total = total + pair_in[n, e].astype(f32)
+            finish_rows(n, fine - 1, fine, total)
 
     @pl.when(freq == 2)
     def _():
@@ -501,6 +544,12 @@
         def block_in(g):
             last_high(g).wait_recv()
 
+        def last_base(o):
+            base[o] = column_product(o, groups - 1, 1, own, spec, 0, outer, low)
+
+        def last_block(g):
+            by_columns(S3, g, 1, own, spec, 0, outer, high, base=base)
+
         loop(0, LEAD, second)
         first_rows(2).wait_recv()
         first_rows(3).start()
@@ -515,6 +564,7 @@
             loop(g, jnp.where(due, g + 1, g), block_in)
             loop(g, jnp.where(due, g + 1, g), block)
 
+        loop(0, halves, last_base)
         loop(LEAD, few, second_more)
         loop(few - 1, few, returned(S1))
 
@@ -523,7 +573,7 @@
             by_rows(S1, c, fine, far, spec1, 0, own, high)
             loop(groups - 1, jnp.where(c == few, groups, groups - 1), block_in)
             by_rows(S2, c, fine, far, spec1, 1, outer, high)
-            loop(groups - 1, jnp.where(c == few, groups, groups - 1), block)
+            loop(groups - 1, jnp.where(c == few, groups, groups - 1), last_block)
 
         loop(few, fine - 1, late)
         c = fine - 1
@@ -538,8 +588,10 @@
             both = held_sum[n] + product(*row_operands(c, fine, far, spec1, n, right, lasts[1]))
             size = both.shape[0] // 2
             put_rows(slot, c, fine, both[:size].astype(bf16), both[size:].astype(bf16))
-        returned(S1)(c)
-        returned(S2)(c)
+            for copy in paired(slot):
+                copy.start()
+        pairs_sent(0, S1)
+        pairs_sent(1, S2)
         for g in range(groups):
             where = cols_of(g)
             await_share(S3, g, where)
@@ -552,12 +604,17 @@
         loop(0, fine, lambda c: first_on(near, c, 3).wait_send())
         loop(0, few, lambda c: second_on(far, c, 3).wait_send())
         settle(S0, fine, fine_rows)
-        settle(S1, fine, fine_rows)
-        settle(S2, fine, fine_rows, few)
+        settle(S1, fine - 1, fine_rows)
+        settle(S2, fine - 1, fine_rows, few)
+        for n, slot in enumerate((S1, S2)):
+            for copy in paired(slot):
+                copy.wait_send()
+            for e in range(groups // pols):
+                pair_on(n, e, line).wait_send()
         settle(S3, groups, cols_of)
         loop(0, fine, lambda c: give_back(S0, c).wait_send())
-        loop(0, fine, lambda c: give_back(S1, c).wait_send())
-        loop(few, fine, lambda c: give_back(S2, c).wait_send())
+        loop(0, fine - 1, lambda c: give_back(S1, c).wait_send())
+        loop(few, fine - 1, lambda c: give_back(S2, c).wait_send())
 
     @pl.when(freq == 3)
     def _():
@@ -625,9 +682,11 @@
             *[pltpu.VMEM((4,) + tile, bf16)] * 2,
             *[pltpu.VMEM((2,) + tile, bf16)] * 2,
             pltpu.VMEM((2, 2 * modes // FINE, modes), f32),
+            pltpu.VMEM((2, modes, local_rows), f32),
+            *[pltpu.VMEM((2, 2, 2, local_rows // FINE, modes), bf16)] * 2,
             dma, dma, dma, *pair(5), *pair(FINE), *pair(max(COARSE, groups)), *pair(groups),
             *pair(FINE), *pair(FINE + 1), *pair(groups),
-            *pair(4, FINE, groups - 1), *pair(4, FINE), *pair(2, COARSE),
+            *pair(4, FINE, groups - 1), *pair(4, FINE), *pair(2, COARSE), *pair(2, 2),
         ],
         compiler_params=pltpu.CompilerParams(
             collective_id=0, has_side_effects=True, vmem_limit_bytes=51 * 2**20
@@ -646,6 +705,7 @@
         and separations == 3
         and lax.axis_size("freq") == separations + 1
         and modes // local_rows == 4
+        and lax.axis_size("pol") == 2
         and local_rows % LANES == 0
         and width % (8 * LANES) == 0
     )

time: 119 us -> 117 us (0.983)
  Pallas kernels: 117 us -> 115 us
    pallas_call x1, Pallas kernels: 117 us -> 115 us  [meet_covariance(): pl.pallas_call(functools.partial(meet_kernel, cut), out_shape=jax.ShapeDt...]
where the time goes in v4:
time: 117 us
  Pallas kernels  115 us (98%)
  other arithmetic  1.41 us (1%)
    pallas_call x1, Pallas kernels, meet_covariance(): pl.pallas_call(functools.partial(meet_kernel, cut), out_shape=jax.ShapeDt...  115 us

profile of v4, /device:TPU:8, one launch (start us, length us, event | category | flops | bytes accessed | tf_op | source)
XLA Modules:
  0.0 116.9 jit_solution(3617186166802713438)
XLA Ops:
  0.0 0.0 copy-start
  0.0 115.5 %shard_map.46 = f32[3,1024,128]{2,1,0:T(8,128)S(1)} custom-call(bf16[2,4,128,2048]{3,2,1,0:T(8,128)(2,1)} %bitcast.11, f32[3,1,2048]{2,1,0:T(1,128)} %bitcast.13, bf16[3,128,512]{2,1,0:T(8,128)(2,1)} %taper_hbm.1), custom_call_target="tpu_custom_call" | custom-call | tf_op jit(solution)/shard_map/pallas_call | solution.py:670
  115.5 0.0 copy-done
  115.5 1.4 %convert_add_fusion = f32[1,3,32,8,512]{4,3,2,1,0:T(8,128)} fusion(f32[1,3,32,8,512]{4,3,2,1,0:T(8,128)S(1)} %bitcast.10, bf16[1,3,32,8,512]{4,3,2,1,0:T(8,128)(2,1)S(1)} %bitcast.12), kind=kLoop, calls=%fused_computation | loop fusion | flops 786432 | bytes 3932160 | tf_op jit(solution)/shard_map/add | solution.py:714
Async XLA Ops:
  0.0 115.5 %copy-start = (bf16[1,3,128,2,512]{4,3,2,1,0:T(2,128)(2,1)S(1)}, bf16[1,3,128,2,512]{4,3,2,1,0:T(2,128)(2,1)}, u32[]{:S(2)}) copy-start(bf16[1,3,128,2,512]{4,3,2,1,0:T(2,128)(2,1)} %param.7) | copy-start | bytes 2359300
